TPU v7x, 32 devices: a whole 2x2x4 slice. The times are simulated.
32 devices in a mesh: blk: 8 (over y, x, core), grp: 4 (over z).
Axes of the slice: x: 2, y: 2, z: 4, core: 2. Of those that a mesh axis runs over, the one named last changes fastest.
Arguments:
- currents: bfloat16 [4, 16, 65536], P('grp', None, 'blk'), may hold values from -6 to 6
- background: float32 [4, 16, 65536], P('grp', None, 'blk'), may hold values from -6 to 6
- green: bfloat16 [4, 512, 8, 128, 128], P('grp', 'blk'), may hold values from -0.1875 to 0.1875
- offsets: int32 [4, 512, 8], P('grp', 'blk'), may hold values from -128 to 128
- station_cells: int32 [2048, 4], P(('blk', 'grp')), may hold values from 0 to 2047, as said below
- station_green: bfloat16 [2048, 4, 128], P(('blk', 'grp')), may hold values from -0.25 to 0.25
- station_background: float32 [16, 2048], P(None, ('blk', 'grp')), may hold values from -6 to 6
Outputs:
- cell_field: float32 [4, 16, 65536], P('grp', None, 'blk')
- station_field: float32 [16, 2048], P(None, ('blk', 'grp'))
Inputs may be any that keep to these rules, and one draw needn't show every extreme that they name: `station_cells`: station s lies with device flat index s // 64; its near blocks lie in blocks from (s // 256 - 1) * 64 to (s // 256 + 2) * 64 - 1, taken modulo 512, in any slab.
All inputs are finite; a program needn't handle non-finite values.
Results may differ from a plain program's by a relative error of at most 0.0003.
Values may be sent and summed in bfloat16 or wider, within the bound.
A program may use at most 64 MiB of HBM per device.

v0:
```python
import jax
import jax.numpy as jnp
from jax import lax
from jax.sharding import PartitionSpec as P

REACH = 2


def from_behind(array, axis, by):
    peers = lax.axis_size(axis)
    return lax.ppermute(array, axis, [(i, (i + by) % peers) for i in range(peers)])


def body(currents, background, green, offsets, station_cells, station_green, station_background):
    local = currents[0]
    n_cols = local.shape[0]
    blocks = green.shape[1]
    cells = green.shape[3]
    span = blocks * cells
    here = lax.axis_index("blk")
    slab_blocks = blocks * lax.axis_size("blk")
    upper = []
    lower = []
    moving = local
    for step in range(REACH):
        moving = from_behind(moving, "blk", -1)
        upper.append(moving)
    moving = local
    for step in range(REACH):
        moving = from_behind(moving, "blk", 1)
        lower.append(moving)
    window = jnp.concatenate(lower[::-1] + [local] + upper, axis=1)
    window_blocks = window.reshape(n_cols, (2 * REACH + 1) * blocks, cells)
    source = jnp.arange(blocks, dtype=jnp.int32)[:, None] + offsets[0] + REACH * blocks
    picked = window_blocks[:, source, :]
    anomalous = jnp.einsum("bkpq,cbkq->cbp", green[0], picked, preferred_element_type=jnp.float32)
    cell_field = background + anomalous.reshape(1, n_cols, span)
    slab_stack = lax.all_gather(currents, "grp", axis=0, tiled=True)
    below = from_behind(slab_stack, "blk", 1)
    above = from_behind(slab_stack, "blk", -1)
    near = jnp.concatenate([below, slab_stack, above], axis=2)
    n_slabs = near.shape[0]
    near_blocks = near.reshape(n_slabs, n_cols, 3 * blocks, cells)
    slab_index = station_cells // slab_blocks
    position = (station_cells % slab_blocks - (here - 1) * blocks) % slab_blocks
    chosen = near_blocks[slab_index, :, position, :]
    station_field = station_background + jnp.einsum(
        "skp,skcp->cs", station_green, chosen, preferred_element_type=jnp.float32
    )
    return (cell_field, station_field)


def solution(mesh):
    return jax.shard_map(
        body,
        mesh=mesh,
        in_specs=(
            P("grp", None, "blk"),
            P("grp", None, "blk"),
            P("grp", "blk", None, None, None),
            P("grp", "blk", None),
            P(("blk", "grp"), None),
            P(("blk", "grp"), None, None),
            P(None, ("blk", "grp")),
        ),
        out_specs=(P("grp", None, "blk"), P(None, ("blk", "grp"))),
        check_vma=False,
    )
```

profile of v0, /device:TPU:1, one launch (start us, length us, event | category | flops | bytes accessed | tf_op | source)
XLA Modules:
  0.0 79.5 jit_solution(7111683563668175119)
XLA Ops:
  7.2 0.7 all-gather.2.cloned.1.call-update
  7.9 2.7 %collective-permute-start = (bf16[16,8192]{1,0:T(8,128)(2,1)}, bf16[16,8192]{1,0:T(8,128)(2,1)S(1)}, u32[]{:S(2)}, u32[]{:S(2)}) collective-permute-start(bf16[16,8192]{1,0:T(8,128)(2,1)} %bitcast.59), channel_id=1, source_target_pairs={{0,4},{4,8},{8,12},{12,16},{16,20},{20,24},{24,28},{28,0},{1,5},{5... | collective-permute-start | bytes 786440 | tf_op jit(solution)/shard_map/ppermute | solution.py:11
  10.6 1.0 %copy.39 = bf16[2,8,64,128]{3,2,1,0:T(8,128)(2,1)S(1)} copy(bf16[2,8,64,128]{3,1,2,0:T(8,128)(2,1)} %bitcast.61) | data formatting | bytes 524288
  11.6 0.7 compare_select_fusion
  12.5 3.5 %collective-permute-done = bf16[16,8192]{1,0:T(8,128)(2,1)S(1)} collective-permute-done((bf16[16,8192]{1,0:T(8,128)(2,1)}, bf16[16,8192]{1,0:T(8,128)(2,1)S(1)}, u32[]{:S(2)}, u32[]{:S(2)}) %collective-permute-start) | collective-permute-done | bytes 262176 | tf_op jit(solution)/shard_map/ppermute | solution.py:11
  16.0 2.4 %collective-permute-start.1 = (bf16[16,8192]{1,0:T(8,128)(2,1)S(1)}, bf16[16,8192]{1,0:T(8,128)(2,1)S(1)}, u32[]{:S(2)}, u32[]{:S(2)}) collective-permute-start(bf16[16,8192]{1,0:T(8,128)(2,1)S(1)} %collective-permute-done), channel_id=1, source_target_pairs={{0,4},{4,8},{8,12},{12,16},{16,20},{20,24},{24,28},{28,0},{1,5},{5... | collective-permute-start | bytes 786440 | tf_op jit(solution)/shard_map/ppermute | solution.py:11
  18.3 0.7 fusion.11
  19.2 0.1 reshape.56
  19.3 3.1 %collective-permute-done.1 = bf16[16,8192]{1,0:T(8,128)(2,1)S(1)} collective-permute-done((bf16[16,8192]{1,0:T(8,128)(2,1)S(1)}, bf16[16,8192]{1,0:T(8,128)(2,1)S(1)}, u32[]{:S(2)}, u32[]{:S(2)}) %collective-permute-start.1) | collective-permute-done | bytes 262176 | tf_op jit(solution)/shard_map/ppermute | solution.py:11
  22.6 0.2 copy_dynamic-update-slice_fusion
  22.9 16.6 %all-gather.2.cloned.1.call-done = bf16[4,16,8192]{2,1,0:T(8,128)(2,1)} async-done(((bf16[1,16,8192]{2,1,0:T(8,128)(2,1)}), bf16[4,16,8192]{2,1,0:T(8,128)(2,1)}) %all-gather.2.cloned.1.call-update) | async-done | bytes 1048592 | tf_op jit(solution)/shard_map/all_gather | solution.py:38
  39.5 1.9 %collective-permute-start.4 = (bf16[4,16,8192]{2,1,0:T(8,128)(2,1)}, bf16[4,16,8192]{2,1,0:T(8,128)(2,1)}, u32[]{:S(2)}, u32[]{:S(2)}) collective-permute-start(bf16[4,16,8192]{2,1,0:T(8,128)(2,1)} %all-gather.2.cloned.1.call-done), channel_id=1, source_target_pairs={{0,4},{4,8},{8,12},{12,16},{16,20},{20,24},{24,28},{28,0},{1,5},{5... | collective-permute-start | bytes 3145736 | tf_op jit(solution)/shard_map/ppermute | solution.py:11
  41.5 2.0 %gather_fusion = bf16[512,16,128]{2,1,0:T(8,128)(2,1)S(1)} fusion(bf16[16,320,128]{2,0,1:T(8,128)(2,1)S(1)} %bitcast_dynamic-update-slice_fusion, s32[1024]{0:T(1024)S(1)} %pad_clamp_fusion), kind=kCustom, calls=%fused_computation | custom fusion | bytes 4196352 | tf_op jit(solution)/shard_map/gather | solution.py:35
  43.5 8.1 %fusion.2 = f32[16,64,128]{2,0,1:T(8,128)S(1)} fusion(bf16[16,64,8,128]{3,0,2,1:T(8,128)(2,1)S(1)} %bitcast.57, bf16[1,64,8,128,128]{4,3,2,1,0:T(8,128)(2,1)} %param.9), kind=kOutput, calls=%fused_computation.6 | convolution fusion | flops 268435456 | bytes 19398656 | tf_op jit(solution)/shard_map/bkpq,cbkq->cbp/dot_general | solution.py:36
  51.6 0.2 copy.28
  51.8 0.1 reshape.46
  51.9 0.8 copy-done.2
  52.6 0.8 %add.79 = f32[1,16,8192]{2,1,0:T(8,128)} add(f32[1,16,8192]{2,1,0:T(8,128)S(1)} %copy-done.2, f32[1,16,8192]{2,1,0:T(8,128)S(1)} %reshape.46) | non-fusion elementwise | flops 131072 | bytes 1572864 | tf_op jit(solution)/shard_map/add | solution.py:37
  53.5 9.4 %collective-permute-done.4 = bf16[4,16,8192]{2,1,0:T(8,128)(2,1)} collective-permute-done((bf16[4,16,8192]{2,1,0:T(8,128)(2,1)}, bf16[4,16,8192]{2,1,0:T(8,128)(2,1)}, u32[]{:S(2)}, u32[]{:S(2)}) %collective-permute-start.4) | collective-permute-done | bytes 1048608 | tf_op jit(solution)/shard_map/ppermute | solution.py:11
  62.9 3.4 %collective-permute-done.5 = bf16[4,16,8192]{2,1,0:T(8,128)(2,1)} collective-permute-done((bf16[4,16,8192]{2,1,0:T(8,128)(2,1)}, bf16[4,16,8192]{2,1,0:T(8,128)(2,1)}, u32[]{:S(2)}, u32[]{:S(2)}) %collective-permute-start.5) | collective-permute-done | bytes 1048608 | tf_op jit(solution)/shard_map/ppermute | solution.py:11
  66.3 1.8 %copy_bitcast_fusion = bf16[4,16,192,128]{3,1,2,0:T(8,128)(2,1)S(1)} fusion(bf16[4,16,8192]{2,1,0:T(8,128)(2,1)} %collective-permute-done.5, bf16[4,16,8192]{2,1,0:T(8,128)(2,1)S(1)} %copy-done.1, bf16[4,16,8192]{2,1,0:T(8,128)(2,1)} %collective-permute-done.4), kind=kLoop, calls=%fused_computation.4 | loop fusion | flops 9437184 | bytes 6291456 | tf_op jit(solution)/shard_map/reshape | solution.py:43
  68.1 2.2 %gather_fusion.1 = bf16[256,16,128]{2,1,0:T(8,128)(2,1)} fusion(bf16[4,16,192,128]{3,1,2,0:T(8,128)(2,1)S(1)} %copy_bitcast_fusion, s32[256]{0:T(256)S(1)} %reshape.56), kind=kCustom, calls=%fused_computation.1 | custom fusion | bytes 2099200 | tf_op jit(solution)/shard_map/gather | solution.py:46
  70.3 1.6 %fusion.5 = f32[64,1,16,1]{2,1,3,0:T(1,128)S(1)} fusion(bf16[64,4,16,128]{3,2,1,0:T(8,128)(2,1)} %bitcast.58, bf16[64,4,128,1]{2,1,0,3:T(4,128)(2,1)S(1)} %bitcast.56), kind=kOutput, calls=%fused_computation.12 | convolution fusion | flops 1048576 | bytes 1118208 | tf_op jit(solution)/shard_map/skp,skcp->cs/dot_general | solution.py:47
  72.0 0.6 bitcast_add_fusion
  (22 shorter events, 0.7 us)
Async XLA Ops:
  7.2 63.2 %copy-start = (bf16[64,4,128]{2,1,0:T(4,128)(2,1)S(1)}, bf16[64,4,128]{2,1,0:T(4,128)(2,1)}, u32[]{:S(2)}) copy-start(bf16[64,4,128]{2,1,0:T(4,128)(2,1)} %param.12) | copy-start | bytes 196612
  7.2 32.3 %all-gather.2.cloned.1.call-start = ((), (), s32[]{:S(2)}) async-start(), calls=%async_computation | async-start | bytes 1310720 | tf_op jit(solution)/shard_map/all_gather | solution.py:38
  7.9 8.1 %collective-permute-start = (bf16[16,8192]{1,0:T(8,128)(2,1)}, bf16[16,8192]{1,0:T(8,128)(2,1)S(1)}, u32[]{:S(2)}, u32[]{:S(2)}) collective-permute-start(bf16[16,8192]{1,0:T(8,128)(2,1)} %bitcast.59), channel_id=1, source_target_pairs={{0,4},{4,8},{8,12},{12,16},{16,20},{20,24},{24,28},{28,0},{1,5},{5... | collective-permute-start | bytes 786440 | tf_op jit(solution)/shard_map/ppermute | solution.py:11
  10.6 8.7 %collective-permute-start.2 = (bf16[16,8192]{1,0:T(8,128)(2,1)}, bf16[16,8192]{1,0:T(8,128)(2,1)S(1)}, u32[]{:S(2)}, u32[]{:S(2)}) collective-permute-start(bf16[16,8192]{1,0:T(8,128)(2,1)} %bitcast.60), channel_id=1, source_target_pairs={{0,28},{4,0},{8,4},{12,8},{16,12},{20,16},{24,20},{28,24},{1,29},{... | collective-permute-start | bytes 786440 | tf_op jit(solution)/shard_map/ppermute | solution.py:11
  16.0 6.5 %collective-permute-start.1 = (bf16[16,8192]{1,0:T(8,128)(2,1)S(1)}, bf16[16,8192]{1,0:T(8,128)(2,1)S(1)}, u32[]{:S(2)}, u32[]{:S(2)}) collective-permute-start(bf16[16,8192]{1,0:T(8,128)(2,1)S(1)} %collective-permute-done), channel_id=1, source_target_pairs={{0,4},{4,8},{8,12},{12,16},{16,20},{20,24},{24,28},{28,0},{1,5},{5... | collective-permute-start | bytes 786440 | tf_op jit(solution)/shard_map/ppermute | solution.py:11
  19.3 22.1 %collective-permute-start.3 = (bf16[16,8192]{1,0:T(8,128)(2,1)S(1)}, bf16[16,8192]{1,0:T(8,128)(2,1)S(1)}, u32[]{:S(2)}, u32[]{:S(2)}) collective-permute-start(bf16[16,8192]{1,0:T(8,128)(2,1)S(1)} %collective-permute-done.2), channel_id=1, source_target_pairs={{0,28},{4,0},{8,4},{12,8},{16,12},{20,16},{24,20},{28,24},{1,29},{... | collective-permute-start | bytes 786440 | tf_op jit(solution)/shard_map/ppermute | solution.py:11
  39.5 23.4 %collective-permute-start.4 = (bf16[4,16,8192]{2,1,0:T(8,128)(2,1)}, bf16[4,16,8192]{2,1,0:T(8,128)(2,1)}, u32[]{:S(2)}, u32[]{:S(2)}) collective-permute-start(bf16[4,16,8192]{2,1,0:T(8,128)(2,1)} %all-gather.2.cloned.1.call-done), channel_id=1, source_target_pairs={{0,4},{4,8},{8,12},{12,16},{16,20},{20,24},{24,28},{28,0},{1,5},{5... | collective-permute-start | bytes 3145736 | tf_op jit(solution)/shard_map/ppermute | solution.py:11
  41.4 24.9 %collective-permute-start.5 = (bf16[4,16,8192]{2,1,0:T(8,128)(2,1)}, bf16[4,16,8192]{2,1,0:T(8,128)(2,1)}, u32[]{:S(2)}, u32[]{:S(2)}) collective-permute-start(bf16[4,16,8192]{2,1,0:T(8,128)(2,1)} %all-gather.2.cloned.1.call-done), channel_id=1, source_target_pairs={{0,28},{4,0},{8,4},{12,8},{16,12},{20,16},{24,20},{28,24},{1,29},{... | collective-permute-start | bytes 3145736 | tf_op jit(solution)/shard_map/ppermute | solution.py:11
  51.6 1.1 %copy-start.2 = (f32[1,16,8192]{2,1,0:T(8,128)S(1)}, f32[1,16,8192]{2,1,0:T(8,128)}, u32[]{:S(2)}) copy-start(f32[1,16,8192]{2,1,0:T(8,128)} %param.8) | copy-start | bytes 1572868
  52.6 13.7 %copy-start.1 = (bf16[4,16,8192]{2,1,0:T(8,128)(2,1)S(1)}, bf16[4,16,8192]{2,1,0:T(8,128)(2,1)}, u32[]{:S(2)}) copy-start(bf16[4,16,8192]{2,1,0:T(8,128)(2,1)} %all-gather.2.cloned.1.call-done) | copy-start | bytes 3145732
  68.1 3.9 %copy-start.3 = (f32[16,64]{1,0:T(8,128)S(1)}, f32[16,64]{1,0:T(8,128)}, u32[]{:S(2)}) copy-start(f32[16,64]{1,0:T(8,128)} %param.13) | copy-start | bytes 12292
Sparse Core Ops, SparseCore 0:
  9.6 29.8 all-gather.1
where the time goes:
time: 79.8 us; the launch traced here: 79.5 us
  waiting for transfers between devices  36.8 us (46%)
  between operations  14.2 us (18%)
  matrix products  9.71 us (12%)
  local copies, waits for them, and re-layouts  7.17 us (9%)
  starting transfers between devices  7.01 us (9%)
  other arithmetic  4.68 us (6%)
    ppermute x6, waiting for transfers between devices, from_behind(): lax.ppermute(array, axis, [(i, (i + by) % peers) for i in range(peers)])  19.5 us
    all_gather x1, waiting for transfers between devices, body(): slab_stack = lax.all_gather(currents, 'grp', axis=0, tiled=True)  16.6 us
    dot_general x1, matrix products, body(): jnp.einsum('bkpq,cbkq->cbp', green[0], picked, preferred_element_type=jnp...  8.07 us
    ppermute x6, starting transfers between devices, from_behind(): lax.ppermute(array, axis, [(i, (i + by) % peers) for i in range(peers)])  6.98 us
    gather x1, local copies, waits for them, and re-layouts, body(): chosen = near_blocks[slab_index, :, position, :]  2.19 us
    unnamed x13, local copies, waits for them, and re-layouts  2.17 us
    gather x1, local copies, waits for them, and re-layouts, body(): picked = window_blocks[:, source, :]  2.02 us
    reshape x1, other arithmetic, body(): near_blocks = near.reshape(n_slabs, n_cols, 3 * blocks, cells)  1.81 us
  transfers between devices with their start and end apart: 7, of which 5 were waited for; matrix products, arithmetic and copies ran while one was open for 18% of the time, Pallas kernels for 0%

commit v1 on v0

--- a/solution.py
+++ b/solution.py
@@ -4,6 +4,28 @@
 from jax.sharding import PartitionSpec as P
 
 REACH = 2
+
+
+def joined_along(pieces, dim):
+    lengths = list(pieces.shape[1:])
+    lengths[dim] *= pieces.shape[0]
+    return jnp.moveaxis(pieces, 0, dim).reshape(lengths)
+
+
+def grow_blocks(array, axis):
+    devices = lax.axis_size(axis)
+    pieces = array[None]
+    for level in range(devices.bit_length() - 1):
+        bit = 1 << level
+        partner_block = lax.ppermute(pieces, axis, [(i, i ^ bit) for i in range(devices)])
+        both = jnp.stack([pieces, partner_block])
+        upper = lax.axis_index(axis) >> level & 1
+        pieces = jnp.where(upper == 0, both, both[::-1]).reshape(-1, *array.shape)
+    return pieces
+
+
+def collect(shard, axis, dim):
+    return joined_along(grow_blocks(shard, axis), dim)
 
 
 def from_behind(array, axis, by):
@@ -35,7 +57,7 @@
     picked = window_blocks[:, source, :]
     anomalous = jnp.einsum("bkpq,cbkq->cbp", green[0], picked, preferred_element_type=jnp.float32)
     cell_field = background + anomalous.reshape(1, n_cols, span)
-    slab_stack = lax.all_gather(currents, "grp", axis=0, tiled=True)
+    slab_stack = collect(currents, "grp", 0)
     below = from_behind(slab_stack, "blk", 1)
     above = from_behind(slab_stack, "blk", -1)
     near = jnp.concatenate([below, slab_stack, above], axis=2)

time: 79.8 us -> 74.6 us (0.935)
  the two profiles are of different devices: /device:TPU:1 before, /device:TPU:0 now
where the time goes in v1:
time: 74.6 us; the launch traced here: 74.2 us
  waiting for transfers between devices  33.8 us (45%)
  starting transfers between devices  12.2 us (16%)
  local copies, waits for them, and re-layouts  12.1 us (16%)
  matrix products  9.7 us (13%)
  other arithmetic  5.6 us (8%)
  between operations  0.79 us (1%)
    ppermute x2, waiting for transfers between devices, grow_blocks(): lax.ppermute(pieces, axis, [(i, i ^ bit) for i in range(devices)])  22.5 us
    ppermute x6, waiting for transfers between devices, from_behind(): lax.ppermute(array, axis, [(i, (i + by) % peers) for i in range(peers)])  11.3 us
    dot_general x1, matrix products, body(): jnp.einsum('bkpq,cbkq->cbp', green[0], picked, preferred_element_type=jnp...  8.06 us
    ppermute x6, starting transfers between devices, from_behind(): lax.ppermute(array, axis, [(i, (i + by) % peers) for i in range(peers)])  7.31 us
    ppermute x2, starting transfers between devices, grow_blocks(): lax.ppermute(pieces, axis, [(i, i ^ bit) for i in range(devices)])  4.92 us
    unnamed x12, local copies, waits for them, and re-layouts  3.63 us
    concatenate x3, local copies, waits for them, and re-layouts, body(): near = jnp.concatenate([below, slab_stack, above], axis=2)  3.49 us
    gather x1, local copies, waits for them, and re-layouts, body(): chosen = near_blocks[slab_index, :, position, :]  2.18 us
  transfers between devices with their start and end apart: 8, of which 5 were waited for; matrix products, arithmetic and copies ran while one was open for 27% of the time, Pallas kernels for 0%

profile of v1, /device:TPU:0, one launch (start us, length us, event | category | flops | bytes accessed | tf_op | source)
XLA Modules:
  0.0 74.2 jit_solution(2370050028861201693)
XLA Ops:
  1.1 2.9 %collective-permute-start.2 = (bf16[16,8192]{1,0:T(8,128)(2,1)}, bf16[16,8192]{1,0:T(8,128)(2,1)S(1)}, u32[]{:S(2)}, u32[]{:S(2)}) collective-permute-start(bf16[16,8192]{1,0:T(8,128)(2,1)} %bitcast.82), channel_id=1, source_target_pairs={{0,28},{4,0},{8,4},{12,8},{16,12},{20,16},{24,20},{28,24},{1,29},{... | collective-permute-start | bytes 786440 | tf_op jit(solution)/shard_map/ppermute | solution.py:33
  4.1 2.3 %collective-permute-start.4 = (bf16[1,1,16,8192]{3,2,1,0:T(8,128)(2,1)}, bf16[1,1,16,8192]{3,2,1,0:T(8,128)(2,1)S(1)}, u32[]{:S(2)}, u32[]{:S(2)}) collective-permute-start(bf16[1,1,16,8192]{3,2,1,0:T(8,128)(2,1)} %bitcast.83), channel_id=1, source_target_pairs={{0,1},{1,0},{2,3},{3,2},{4,5},{5,4},{6,7},{7,6},{8,9},{9,8},{10,11... | collective-permute-start | bytes 786440 | tf_op jit(solution)/shard_map/ppermute | solution.py:20
  6.4 0.7 fusion.13
  7.3 1.0 %copy.33 = bf16[2,8,64,128]{3,2,1,0:T(8,128)(2,1)S(1)} copy(bf16[2,8,64,128]{3,1,2,0:T(8,128)(2,1)} %bitcast.84) | data formatting | bytes 524288
  8.3 0.7 compare_select_fusion
  9.2 3.0 %collective-permute-done.4 = bf16[1,1,16,8192]{3,2,1,0:T(8,128)(2,1)S(1)} collective-permute-done((bf16[1,1,16,8192]{3,2,1,0:T(8,128)(2,1)}, bf16[1,1,16,8192]{3,2,1,0:T(8,128)(2,1)S(1)}, u32[]{:S(2)}, u32[]{:S(2)}) %collective-permute-start.4) | collective-permute-done | bytes 262176 | tf_op jit(solution)/shard_map/ppermute | solution.py:20
  12.2 1.0 %pad_maximum_fusion.2 = bf16[2,1,1,16,8192]{4,3,2,1,0:T(8,128)(2,1)S(1)} fusion(bf16[1,1,1,16,8192]{4,3,2,1,0:T(8,128)(2,1)S(1)} %bitcast.87, bf16[1,1,1,16,8192]{4,3,2,1,0:T(8,128)(2,1)} %bitcast.85), kind=kLoop, calls=%fused_computation.11 | loop fusion | flops 262144 | bytes 1048576 | tf_op jit(solution)/shard_map/stack | solution.py:21
  13.4 2.7 %collective-permute-start.5 = (bf16[2,1,16,8192]{3,2,0,1:T(8,128)(2,1)S(1)}, bf16[2,1,16,8192]{3,2,0,1:T(8,128)(2,1)S(1)}, u32[]{:S(2)}, u32[]{:S(2)}) collective-permute-start(bf16[2,1,16,8192]{3,2,0,1:T(8,128)(2,1)S(1)} %get-tuple-element.3), channel_id=1, source_target_pairs={{0,2},{1,3},{2,0},{3,1},{4,6},{5,7},{6,4},{7,5},{8,10},{9,11},{10,... | collective-permute-start | bytes 1572872 | tf_op jit(solution)/shard_map/ppermute | solution.py:20
  16.0 2.3 %collective-permute-start.3 = (bf16[16,8192]{1,0:T(8,128)(2,1)S(1)}, bf16[16,8192]{1,0:T(8,128)(2,1)S(1)}, u32[]{:S(2)}, u32[]{:S(2)}) collective-permute-start(bf16[16,8192]{1,0:T(8,128)(2,1)S(1)} %collective-permute-done.2), channel_id=1, source_target_pairs={{0,28},{4,0},{8,4},{12,8},{16,12},{20,16},{24,20},{28,24},{1,29},{... | collective-permute-start | bytes 786440 | tf_op jit(solution)/shard_map/ppermute | solution.py:33
  18.4 1.6 %collective-permute-done.1 = bf16[16,8192]{1,0:T(8,128)(2,1)S(1)} collective-permute-done((bf16[16,8192]{1,0:T(8,128)(2,1)S(1)}, bf16[16,8192]{1,0:T(8,128)(2,1)S(1)}, u32[]{:S(2)}, u32[]{:S(2)}) %collective-permute-start.1) | collective-permute-done | bytes 262176 | tf_op jit(solution)/shard_map/ppermute | solution.py:33
  20.3 19.5 %collective-permute-done.5 = bf16[2,1,16,8192]{3,2,0,1:T(8,128)(2,1)S(1)} collective-permute-done((bf16[2,1,16,8192]{3,2,0,1:T(8,128)(2,1)S(1)}, bf16[2,1,16,8192]{3,2,0,1:T(8,128)(2,1)S(1)}, u32[]{:S(2)}, u32[]{:S(2)}) %collective-permute-start.5) | collective-permute-done | bytes 524320 | tf_op jit(solution)/shard_map/ppermute | solution.py:20
  39.9 1.1 %reverse_select_fusion = bf16[2,2,1,16,8192]{4,3,1,2,0:T(8,128)(2,1)} fusion(bf16[2,2,1,16,8192]{4,3,1,2,0:T(8,128)(2,1)S(1)} %pad_maximum_fusion.1, pred[]{:T(512)S(6)} %eq.9), kind=kLoop, calls=%fused_computation.5 | loop fusion | flops 524288 | bytes 2097153 | tf_op jit(solution)/shard_map/jit(_where)/select_n | solution.py:23
  41.0 1.4 %collective-permute-start.7 = (bf16[4,16,8192]{2,1,0:T(8,128)(2,1)}, bf16[4,16,8192]{2,1,0:T(8,128)(2,1)}, u32[]{:S(2)}, u32[]{:S(2)}) collective-permute-start(bf16[4,16,8192]{2,1,0:T(8,128)(2,1)} %bitcast.14), channel_id=1, source_target_pairs={{0,28},{4,0},{8,4},{12,8},{16,12},{20,16},{24,20},{28,24},{1,29},{... | collective-permute-start | bytes 3145736 | tf_op jit(solution)/shard_map/ppermute | solution.py:33
  42.5 2.0 %gather_fusion = bf16[512,16,128]{2,1,0:T(8,128)(2,1)S(1)} fusion(bf16[16,320,128]{2,0,1:T(8,128)(2,1)S(1)} %bitcast_dynamic-update-slice_fusion, s32[1024]{0:T(1024)S(1)} %pad_clamp_fusion), kind=kCustom, calls=%fused_computation | custom fusion | bytes 4196352 | tf_op jit(solution)/shard_map/gather | solution.py:57
  44.6 8.1 %fusion.2 = f32[16,64,128]{2,0,1:T(8,128)S(1)} fusion(bf16[16,64,8,128]{3,0,2,1:T(8,128)(2,1)S(1)} %bitcast.77, bf16[1,64,8,128,128]{4,3,2,1,0:T(8,128)(2,1)} %param.9), kind=kOutput, calls=%fused_computation.6 | convolution fusion | flops 268435456 | bytes 19398656 | tf_op jit(solution)/shard_map/bkpq,cbkq->cbp/dot_general | solution.py:58
  53.0 0.8 %copy-done.1 = f32[1,16,8192]{2,1,0:T(8,128)S(1)} copy-done((f32[1,16,8192]{2,1,0:T(8,128)S(1)}, f32[1,16,8192]{2,1,0:T(8,128)}, u32[]{:S(2)}) %copy-start.1) | copy-done | bytes 524312
  53.7 0.8 %add.79 = f32[1,16,8192]{2,1,0:T(8,128)} add(f32[1,16,8192]{2,1,0:T(8,128)S(1)} %copy-done.1, f32[1,16,8192]{2,1,0:T(8,128)S(1)} %reshape.51) | non-fusion elementwise | flops 131072 | bytes 1572864 | tf_op jit(solution)/shard_map/add | solution.py:59
  54.6 1.5 %copy.34 = bf16[8,8,64,128]{3,2,1,0:T(8,128)(2,1)S(1)} copy(bf16[8,8,64,128]{3,1,2,0:T(8,128)(2,1)} %bitcast.41) | data formatting | bytes 2097152
  56.8 7.3 %collective-permute-done.7 = bf16[4,16,8192]{2,1,0:T(8,128)(2,1)} collective-permute-done((bf16[4,16,8192]{2,1,0:T(8,128)(2,1)}, bf16[4,16,8192]{2,1,0:T(8,128)(2,1)}, u32[]{:S(2)}, u32[]{:S(2)}) %collective-permute-start.7) | collective-permute-done | bytes 1048608 | tf_op jit(solution)/shard_map/ppermute | solution.py:33
  64.1 1.4 %copy_bitcast_fusion = bf16[4,16,64,128]{3,1,2,0:T(8,128)(2,1)S(1)} fusion(bf16[4,16,8192]{2,1,0:T(8,128)(2,1)} %collective-permute-done.7), kind=kLoop, calls=%fused_computation.7 | loop fusion | bytes 2097152 | tf_op jit(solution)/shard_map/concatenate | solution.py:63
  65.5 2.4 %collective-permute-done.6 = bf16[4,16,8192]{2,1,0:T(8,128)(2,1)} collective-permute-done((bf16[4,16,8192]{2,1,0:T(8,128)(2,1)}, bf16[4,16,8192]{2,1,0:T(8,128)(2,1)}, u32[]{:S(2)}, u32[]{:S(2)}) %collective-permute-start.6) | collective-permute-done | bytes 1048608 | tf_op jit(solution)/shard_map/ppermute | solution.py:33
  67.9 1.4 %copy_bitcast_fusion.1 = bf16[4,16,64,128]{3,1,2,0:T(8,128)(2,1)S(1)} fusion(bf16[4,16,8192]{2,1,0:T(8,128)(2,1)} %collective-permute-done.6), kind=kLoop, calls=%fused_computation.8 | loop fusion | bytes 2097152 | tf_op jit(solution)/shard_map/concatenate | solution.py:63
  69.7 2.2 %gather_fusion.1 = bf16[256,16,128]{2,1,0:T(8,128)(2,1)} fusion(bf16[4,16,192,128]{3,1,2,0:T(8,128)(2,1)S(1)} %pad_maximum_fusion, s32[256]{0:T(256)S(1)} %reshape.61), kind=kCustom, calls=%fused_computation.1 | custom fusion | bytes 2099200 | tf_op jit(solution)/shard_map/gather | solution.py:68
  71.9 1.6 %fusion.7 = f32[64,1,16,1]{2,1,3,0:T(1,128)S(1)} fusion(bf16[64,4,16,128]{3,2,1,0:T(8,128)(2,1)} %bitcast.79, bf16[64,4,128,1]{2,1,0,3:T(4,128)(2,1)S(1)} %bitcast.76), kind=kOutput, calls=%fused_computation.19 | convolution fusion | flops 1048576 | bytes 1118208 | tf_op jit(solution)/shard_map/skp,skcp->cs/dot_general | solution.py:69
  (29 shorter events, 3.7 us)
Async XLA Ops:
  0.6 71.2 %copy-start = (bf16[64,4,128]{2,1,0:T(4,128)(2,1)S(1)}, bf16[64,4,128]{2,1,0:T(4,128)(2,1)}, u32[]{:S(2)}) copy-start(bf16[64,4,128]{2,1,0:T(4,128)(2,1)} %param.12) | copy-start | bytes 196612
  0.6 12.5 %collective-permute-start = (bf16[16,8192]{1,0:T(8,128)(2,1)}, bf16[16,8192]{1,0:T(8,128)(2,1)S(1)}, u32[]{:S(2)}, u32[]{:S(2)}) collective-permute-start(bf16[16,8192]{1,0:T(8,128)(2,1)} %bitcast.81), channel_id=1, source_target_pairs={{0,4},{4,8},{8,12},{12,16},{16,20},{20,24},{24,28},{28,0},{1,5},{5... | collective-permute-start | bytes 786440 | tf_op jit(solution)/shard_map/ppermute | solution.py:33
  1.1 14.9 %collective-permute-start.2 = (bf16[16,8192]{1,0:T(8,128)(2,1)}, bf16[16,8192]{1,0:T(8,128)(2,1)S(1)}, u32[]{:S(2)}, u32[]{:S(2)}) collective-permute-start(bf16[16,8192]{1,0:T(8,128)(2,1)} %bitcast.82), channel_id=1, source_target_pairs={{0,28},{4,0},{8,4},{12,8},{16,12},{20,16},{24,20},{28,24},{1,29},{... | collective-permute-start | bytes 786440 | tf_op jit(solution)/shard_map/ppermute | solution.py:33
  4.1 8.1 %collective-permute-start.4 = (bf16[1,1,16,8192]{3,2,1,0:T(8,128)(2,1)}, bf16[1,1,16,8192]{3,2,1,0:T(8,128)(2,1)S(1)}, u32[]{:S(2)}, u32[]{:S(2)}) collective-permute-start(bf16[1,1,16,8192]{3,2,1,0:T(8,128)(2,1)} %bitcast.83), channel_id=1, source_target_pairs={{0,1},{1,0},{2,3},{3,2},{4,5},{5,4},{6,7},{7,6},{8,9},{9,8},{10,11... | collective-permute-start | bytes 786440 | tf_op jit(solution)/shard_map/ppermute | solution.py:20
  13.2 6.7 %collective-permute-start.1 = (bf16[16,8192]{1,0:T(8,128)(2,1)S(1)}, bf16[16,8192]{1,0:T(8,128)(2,1)S(1)}, u32[]{:S(2)}, u32[]{:S(2)}) collective-permute-start(bf16[16,8192]{1,0:T(8,128)(2,1)S(1)} %collective-permute-done), channel_id=1, source_target_pairs={{0,4},{4,8},{8,12},{12,16},{16,20},{20,24},{24,28},{28,0},{1,5},{5... | collective-permute-start | bytes 786440 | tf_op jit(solution)/shard_map/ppermute | solution.py:33
  13.4 26.4 %collective-permute-start.5 = (bf16[2,1,16,8192]{3,2,0,1:T(8,128)(2,1)S(1)}, bf16[2,1,16,8192]{3,2,0,1:T(8,128)(2,1)S(1)}, u32[]{:S(2)}, u32[]{:S(2)}) collective-permute-start(bf16[2,1,16,8192]{3,2,0,1:T(8,128)(2,1)S(1)} %get-tuple-element.3), channel_id=1, source_target_pairs={{0,2},{1,3},{2,0},{3,1},{4,6},{5,7},{6,4},{7,5},{8,10},{9,11},{10,... | collective-permute-start | bytes 1572872 | tf_op jit(solution)/shard_map/ppermute | solution.py:20
  16.0 26.4 %collective-permute-start.3 = (bf16[16,8192]{1,0:T(8,128)(2,1)S(1)}, bf16[16,8192]{1,0:T(8,128)(2,1)S(1)}, u32[]{:S(2)}, u32[]{:S(2)}) collective-permute-start(bf16[16,8192]{1,0:T(8,128)(2,1)S(1)} %collective-permute-done.2), channel_id=1, source_target_pairs={{0,28},{4,0},{8,4},{12,8},{16,12},{20,16},{24,20},{28,24},{1,29},{... | collective-permute-start | bytes 786440 | tf_op jit(solution)/shard_map/ppermute | solution.py:33
  41.0 23.0 %collective-permute-start.7 = (bf16[4,16,8192]{2,1,0:T(8,128)(2,1)}, bf16[4,16,8192]{2,1,0:T(8,128)(2,1)}, u32[]{:S(2)}, u32[]{:S(2)}) collective-permute-start(bf16[4,16,8192]{2,1,0:T(8,128)(2,1)} %bitcast.14), channel_id=1, source_target_pairs={{0,28},{4,0},{8,4},{12,8},{16,12},{20,16},{24,20},{28,24},{1,29},{... | collective-permute-start | bytes 3145736 | tf_op jit(solution)/shard_map/ppermute | solution.py:33
  44.5 23.3 %collective-permute-start.6 = (bf16[4,16,8192]{2,1,0:T(8,128)(2,1)}, bf16[4,16,8192]{2,1,0:T(8,128)(2,1)}, u32[]{:S(2)}, u32[]{:S(2)}) collective-permute-start(bf16[4,16,8192]{2,1,0:T(8,128)(2,1)} %bitcast.14), channel_id=1, source_target_pairs={{0,4},{4,8},{8,12},{12,16},{16,20},{20,24},{24,28},{28,0},{1,5},{5... | collective-permute-start | bytes 3145736 | tf_op jit(solution)/shard_map/ppermute | solution.py:33
  52.7 1.1 %copy-start.1 = (f32[1,16,8192]{2,1,0:T(8,128)S(1)}, f32[1,16,8192]{2,1,0:T(8,128)}, u32[]{:S(2)}) copy-start(f32[1,16,8192]{2,1,0:T(8,128)} %param.8) | copy-start | bytes 1572868
  69.7 3.9 %copy-start.2 = (f32[16,64]{1,0:T(8,128)S(1)}, f32[16,64]{1,0:T(8,128)}, u32[]{:S(2)}) copy-start(f32[16,64]{1,0:T(8,128)} %param.13) | copy-start | bytes 12292
